TPU v7x, 32 devices: a whole 2x2x4 slice. The times are simulated.
32 devices in a mesh: pair: 4 (over x, core), box: 8 (over z, y).
Axes of the slice: x: 2, y: 2, z: 4, core: 2. Of those that a mesh axis runs over, the one named last changes fastest.
Arguments:
- sources: bfloat16 [3072, 64, 256], P(('pair', 'box')), may hold values from -6 to 6
- basis_in: bfloat16 [3072, 4096], P(('pair', 'box')), may hold values from -0.75 to 0.75
- kinds: int32 [5, 3072], P(None, ('pair', 'box')), may hold values from 0 to 7
- couplings: bfloat16 [5, 8, 64, 128], replicated, may hold values from -0.5 to 0.5
- basis_out: bfloat16 [3072, 4096], P(('pair', 'box')), may hold values from -0.75 to 0.75
Outputs:
- wavefield: bfloat16 [3072, 64, 256], P(('pair', 'box'))
Inputs may be any that keep to these rules, and one draw needn't show every extreme that they name: Row l of kinds is indexed by source node for l < 2 and by target position for later levels.
All inputs are finite; a program needn't handle non-finite values.
Results may differ from a plain program's by a relative error of at most 0.015.
Values may be sent and summed in bfloat16 or wider, within the bound.
A program may use at most 192 MiB of HBM per device.

v0:
```python
import jax
import jax.numpy as jnp
from jax import lax
from jax.sharding import PartitionSpec as P


def from_partner(value, axis, stride):
    mask = 2**stride
    pairs = [(source, source ^ mask) for source in range(lax.axis_size(axis))]
    return lax.ppermute(value, axis, pairs)


def butterfly_level(coeffs, weights, stride):
    leading = coeffs.shape[0]
    groups = leading // (2 * stride)
    shaped = coeffs.reshape((groups, 2, stride) + coeffs.shape[1:])
    stacked = jnp.concatenate([shaped[:, 0], shaped[:, 1]], axis=-2)
    paired = weights.reshape((groups, 2, stride) + weights.shape[1:])
    product = jnp.einsum(
        "htlkij,hlkjs->htlkis", paired, stacked, preferred_element_type=jnp.float32
    )
    return product.astype(jnp.bfloat16).reshape(coeffs.shape)


def body(sources, basis_in, kinds, couplings, basis_out):
    pair_size = lax.axis_size("pair")
    box_size = lax.axis_size("box")
    pair_index = lax.axis_index("pair")
    box_count = sources.shape[0]
    points = sources.shape[1]
    shots = sources.shape[2]
    rank = couplings.shape[2]
    pair_levels = pair_size.bit_length() - 1
    box_levels = box_size.bit_length() - 1
    coeffs = jnp.einsum(
        "kpr,kps->krs",
        basis_in.reshape(box_count, points, rank),
        sources,
        preferred_element_type=jnp.float32,
    ).astype(jnp.bfloat16)
    for depth_bit in range(pair_levels):
        partner_coeffs = from_partner(coeffs, "pair", depth_bit)
        upper_half = pair_index >> depth_bit & 1 == 1
        first_child = jnp.where(upper_half, partner_coeffs, coeffs)
        second_child = jnp.where(upper_half, coeffs, partner_coeffs)
        stacked = jnp.concatenate([first_child, second_child], axis=1)
        weights = couplings[depth_bit][kinds[depth_bit]]
        coeffs = jnp.einsum(
            "kij,kjs->kis", weights, stacked, preferred_element_type=jnp.float32
        ).astype(jnp.bfloat16)
    group_size = box_count // box_size
    moved = lax.all_to_all(
        coeffs.reshape(box_size, group_size, rank, shots),
        "box",
        split_axis=0,
        concat_axis=0,
        tiled=True,
    )
    for depth_bit in range(box_levels):
        level_row = pair_levels + depth_bit
        kind_rows = kinds[level_row].reshape(box_size, group_size)
        moved = butterfly_level(moved, couplings[level_row][kind_rows], 2**depth_bit)
    wavefield = jnp.einsum(
        "tpr,trs->tps",
        basis_out.reshape(box_count, points, rank),
        moved.reshape(box_count, rank, shots),
        preferred_element_type=jnp.float32,
    )
    return wavefield.astype(jnp.bfloat16)


def solution(mesh):
    in_specs = (
        P(("pair", "box"), None, None),
        P(("pair", "box"), None),
        P(None, ("pair", "box")),
        P(),
        P(("pair", "box"), None),
    )
    out_specs = P(("pair", "box"), None, None)
    return jax.shard_map(body, mesh=mesh, in_specs=in_specs, out_specs=out_specs, check_vma=False)
```

profile of v0, /device:TPU:0, one launch (start us, length us, event | category | flops | bytes accessed | tf_op | source)
XLA Modules:
  0.0 188.3 jit_solution(10971405954136450859)
XLA Ops:
  0.0 0.0 copy-start
  0.0 2.4 %copy.12 = bf16[96,4096]{0,1:T(8,128)(2,1)} copy(bf16[96,4096]{1,0:T(8,128)(2,1)} %param.6) | data formatting | bytes 1572864 | tf_op args[1]
  2.4 4.8 %copy.13 = bf16[96,64,64]{1,2,0:T(8,128)(2,1)} copy(bf16[96,64,64]{0,2,1:T(8,128)(2,1)} %bitcast.95) | data formatting | bytes 1572864 | tf_op jit(solution)/shard_map/reshape | solution.py:37
  7.1 0.0 copy-done
  7.1 0.0 copy-start.7
  7.1 4.0 %convolution_convert_fusion = bf16[96,64,256]{2,1,0:T(8,128)(2,1)} fusion(bf16[96,64,64]{1,2,0:T(8,128)(2,1)} %copy.13, bf16[96,64,256]{2,1,0:T(8,128)(2,1)S(1)} %copy-done), kind=kOutput, calls=%fused_computation.32 | convolution fusion | flops 202899456 | bytes 7077888 | tf_op jit(solution)/shard_map/kpr,kps->krs/dot_general | solution.py:35
  11.2 0.5 collective-permute-start
  11.6 0.0 copy-done.7
  11.7 1.2 slice_bitcast_fusion.4
  12.9 0.8 gather_fusion.1
  13.7 3.5 %collective-permute-done = bf16[96,64,256]{2,1,0:T(8,128)(2,1)} collective-permute-done((bf16[96,64,256]{2,1,0:T(8,128)(2,1)}, bf16[96,64,256]{2,1,0:T(8,128)(2,1)}, u32[]{:S(2)}, u32[]{:S(2)}) %collective-permute-start) | collective-permute-done | bytes 3145760 | tf_op jit(solution)/shard_map/ppermute | solution.py:10
  17.3 3.3 %broadcast_select_fusion.1 = (bf16[96,64,256]{2,1,0:T(8,128)(2,1)S(1)}, bf16[96,64,256]{2,1,0:T(8,128)(2,1)S(1)}) fusion(bf16[96,64,256]{2,1,0:T(8,128)(2,1)} %collective-permute-done, bf16[96,64,256]{2,1,0:T(8,128)(2,1)} %convolution_convert_fusion, pred[]{:T(512)S(6)} %eq.7), kind=kLoop, calls=%fused_computation.29 | loop fusion | flops 3145728 | bytes 12582913 | tf_op jit(solution)/shard_map/jit(_where)/select_n | solution.py:44
  20.5 2.3 %fusion.21 = bf16[96,64,256]{2,1,0:T(8,128)(2,1)} fusion(bf16[96,64,128]{2,1,0:T(8,128)(2,1)S(1)} %gather_fusion.1, bf16[96,64,256]{2,1,0:T(8,128)(2,1)S(1)} %get-tuple-element.11, bf16[96,64,256]{2,1,0:T(8,128)(2,1)S(1)} %get-tuple-element.10), kind=kOutput, calls=%fused_computation.35 | convolution fusion | flops 416808960 | bytes 11010048 | tf_op jit(solution)/shard_map/kij,kjs->kis/dot_general | solution.py:48
  22.9 2.9 %collective-permute-start.1 = (bf16[96,64,256]{2,1,0:T(8,128)(2,1)}, bf16[96,64,256]{2,1,0:T(8,128)(2,1)}, u32[]{:S(2)}, u32[]{:S(2)}) collective-permute-start(bf16[96,64,256]{2,1,0:T(8,128)(2,1)} %fusion.21), channel_id=1, source_target_pairs={{0,16},{8,24},{16,0},{24,8},{1,17},{9,25},{17,1},{25,9},{2,18},{10... | collective-permute-start | bytes 9437192 | tf_op jit(solution)/shard_map/ppermute | solution.py:10
  25.7 0.8 gather_fusion
  26.6 67.8 %collective-permute-done.1 = bf16[96,64,256]{2,1,0:T(8,128)(2,1)} collective-permute-done((bf16[96,64,256]{2,1,0:T(8,128)(2,1)}, bf16[96,64,256]{2,1,0:T(8,128)(2,1)}, u32[]{:S(2)}, u32[]{:S(2)}) %collective-permute-start.1) | collective-permute-done | bytes 3145760 | tf_op jit(solution)/shard_map/ppermute | solution.py:10
  94.4 3.3 %broadcast_select_fusion.3 = (bf16[96,64,256]{2,1,0:T(8,128)(2,1)S(1)}, bf16[96,64,256]{2,1,0:T(8,128)(2,1)S(1)}) fusion(bf16[96,64,256]{2,1,0:T(8,128)(2,1)} %collective-permute-done.1, bf16[96,64,256]{2,1,0:T(8,128)(2,1)} %fusion.21, pred[]{:T(512)S(6)} %eq.6), kind=kLoop, calls=%fused_computation.31 | loop fusion | flops 3145728 | bytes 12582913 | tf_op jit(solution)/shard_map/jit(_where)/select_n | solution.py:44
  97.7 2.3 %fusion.18 = bf16[96,64,256]{2,1,0:T(8,128)(2,1)} fusion(bf16[96,64,128]{2,1,0:T(8,128)(2,1)S(1)} %gather_fusion, bf16[96,64,256]{2,1,0:T(8,128)(2,1)S(1)} %get-tuple-element.9, bf16[96,64,256]{2,1,0:T(8,128)(2,1)S(1)} %get-tuple-element.8), kind=kOutput, calls=%fused_computation.34 | convolution fusion | flops 416808960 | bytes 11010048 | tf_op jit(solution)/shard_map/kij,kjs->kis/dot_general | solution.py:48
  100.0 6.1 %all-to-all-start = ((bf16[8,12,64,256]{3,2,1,0:T(8,128)(2,1)}), bf16[8,12,64,256]{3,2,1,0:T(8,128)(2,1)S(1)}, u32[]{:S(2)}, u32[]{:S(2)}) async-start(bf16[8,12,64,256]{3,2,1,0:T(8,128)(2,1)} %bitcast.97), calls=%async_computation | async-start | bytes 6291456 | tf_op jit(solution)/shard_map/all_to_all | solution.py:52
  106.1 0.6 slice_reduce_fusion
  106.7 0.1 reshape_squeeze.9
  106.8 0.1 reshape.202
  106.9 0.1 reshape_squeeze.10
  106.9 0.1 reshape.210
  107.0 0.7 reshape_squeeze.11
  107.7 0.7 reshape.218
  108.4 2.2 %copy.23 = bf16[96,4096]{0,1:T(8,128)(2,1)} copy(bf16[96,4096]{1,0:T(8,128)(2,1)} %param.9) | data formatting | bytes 1572864 | tf_op args[4]
  110.7 4.1 %copy.24 = bf16[96,64,64]{2,1,0:T(8,128)(2,1)} copy(bf16[96,64,64]{0,2,1:T(8,128)(2,1)} %bitcast.96) | data formatting | bytes 1572864 | tf_op jit(solution)/shard_map/reshape | solution.py:65
  114.7 0.0 copy-start.6
  114.7 1.9 %gather_fusion.2 = bf16[96,64,128]{2,1,0:T(8,128)(2,1)} fusion(bf16[8,64,128]{2,1,0:T(8,128)(2,1)S(1)} %get-tuple-element.19, s32[1024]{0:T(1024)S(1)} %pad_clamp_fusion.2), kind=kCustom, calls=%fused_computation.2 | custom fusion | bytes 3146112 | tf_op jit(solution)/shard_map/gather | solution.py:62
  116.7 1.9 %gather_fusion.3 = bf16[96,64,128]{2,1,0:T(8,128)(2,1)} fusion(bf16[8,64,128]{2,1,0:T(8,128)(2,1)S(1)} %get-tuple-element.22, s32[1024]{0:T(1024)S(1)} %pad_clamp_fusion.1), kind=kCustom, calls=%fused_computation.3 | custom fusion | bytes 3146112 | tf_op jit(solution)/shard_map/gather | solution.py:62
  118.6 0.0 copy-done.6
  118.6 2.0 %gather_fusion.4 = bf16[96,64,128]{2,1,0:T(8,128)(2,1)} fusion(bf16[8,64,128]{2,1,0:T(8,128)(2,1)S(1)} %get-tuple-element.18, s32[1024]{0:T(1024)S(1)} %pad_clamp_fusion), kind=kCustom, calls=%fused_computation.4 | custom fusion | bytes 3146112 | tf_op jit(solution)/shard_map/gather | solution.py:62
  120.6 55.7 %all-to-all-done = bf16[8,12,64,256]{3,2,1,0:T(8,128)(2,1)S(1)} async-done(((bf16[8,12,64,256]{3,2,1,0:T(8,128)(2,1)}), bf16[8,12,64,256]{3,2,1,0:T(8,128)(2,1)S(1)}, u32[]{:S(2)}, u32[]{:S(2)}) %all-to-all-start) | async-done | bytes 3145760 | tf_op jit(solution)/shard_map/all_to_all | solution.py:52
  176.3 0.0 copy-start.5
  176.3 0.2 slice_bitcast_fusion.3
  176.5 1.2 copy-done.5
  177.7 1.0 fusion.17
  178.7 0.4 fusion.34
  179.1 0.0 copy-start.4
  179.1 0.4 copy_bitcast_fusion
  179.5 1.0 copy-done.4
  180.5 1.0 convert_bitcast_fusion.2
  181.4 0.4 copy.20
  181.9 0.0 copy-start.3
  181.9 0.4 slice_bitcast_fusion.1
  182.3 1.0 copy-done.3
  183.3 1.0 convert_bitcast_fusion.1
  184.2 0.0 copy-start.2
  184.3 0.4 copy.22
  184.7 0.0 copy-start.1
  184.7 1.0 copy-done.2
  185.7 2.6 %convert_bitcast_fusion = bf16[96,64,256]{2,1,0:T(8,128)(2,1)} fusion(bf16[96,64,64]{2,1,0:T(8,128)(2,1)S(1)} %copy-done.2, bf16[96,64,256]{2,1,0:T(8,128)(2,1)S(1)} %bitcast.93), kind=kOutput, calls=%fused_computation.25 | convolution fusion | flops 202899456 | bytes 7077888 | tf_op jit(solution)/shard_map/tpr,trs->tps/dot_general | solution.py:63
  188.3 0.0 copy-done.1
  (9 shorter events, 0.1 us)
Async XLA Ops:
  0.0 7.1 %copy-start = (bf16[96,64,256]{2,1,0:T(8,128)(2,1)S(1)}, bf16[96,64,256]{2,1,0:T(8,128)(2,1)}, u32[]{:S(2)}) copy-start(bf16[96,64,256]{2,1,0:T(8,128)(2,1)} %param.5) | copy-start | bytes 9437188
  7.1 4.5 %copy-start.7 = (s32[5,96]{1,0:T(8,128)S(1)}, s32[5,96]{1,0:T(8,128)}, u32[]{:S(2)}) copy-start(s32[5,96]{1,0:T(8,128)} %param.7) | copy-start | bytes 5764
  11.2 6.1 %collective-permute-start = (bf16[96,64,256]{2,1,0:T(8,128)(2,1)}, bf16[96,64,256]{2,1,0:T(8,128)(2,1)}, u32[]{:S(2)}, u32[]{:S(2)}) collective-permute-start(bf16[96,64,256]{2,1,0:T(8,128)(2,1)} %convolution_convert_fusion), channel_id=1, source_target_pairs={{0,8},{8,0},{16,24},{24,16},{1,9},{9,1},{17,25},{25,17},{2,10},{10... | collective-permute-start | bytes 9437192 | tf_op jit(solution)/shard_map/ppermute | solution.py:10
  22.9 71.6 %collective-permute-start.1 = (bf16[96,64,256]{2,1,0:T(8,128)(2,1)}, bf16[96,64,256]{2,1,0:T(8,128)(2,1)}, u32[]{:S(2)}, u32[]{:S(2)}) collective-permute-start(bf16[96,64,256]{2,1,0:T(8,128)(2,1)} %fusion.21), channel_id=1, source_target_pairs={{0,16},{8,24},{16,0},{24,8},{1,17},{9,25},{17,1},{25,9},{2,18},{10... | collective-permute-start | bytes 9437192 | tf_op jit(solution)/shard_map/ppermute | solution.py:10
  100.0 76.3 %all-to-all-start = ((bf16[8,12,64,256]{3,2,1,0:T(8,128)(2,1)}), bf16[8,12,64,256]{3,2,1,0:T(8,128)(2,1)S(1)}, u32[]{:S(2)}, u32[]{:S(2)}) async-start(bf16[8,12,64,256]{3,2,1,0:T(8,128)(2,1)} %bitcast.97), calls=%async_computation | async-start | bytes 6291456 | tf_op jit(solution)/shard_map/all_to_all | solution.py:52
  114.7 3.9 %copy-start.6 = (s32[96]{0:T(128)S(1)}, s32[96]{0:T(128)}, u32[]{:S(2)}) copy-start(s32[96]{0:T(128)} %reshape.218) | copy-start | bytes 1156
  176.3 1.4 copy-start.5
  179.1 1.4 copy-start.4
  181.9 1.4 copy-start.3
  184.2 1.4 copy-start.2
  184.7 3.6 %copy-start.1 = (bf16[96,64,256]{2,1,0:T(8,128)(2,1)S(1)}, bf16[96,64,256]{2,1,0:T(8,128)(2,1)}, u32[]{:S(2)}) copy-start(bf16[96,64,256]{2,1,0:T(8,128)(2,1)} %param.5) | copy-start | bytes 9437188
where the time goes:
time: 189 us; the launch traced here: 188 us
  waiting for transfers between devices  127 us (67%)
  local copies, waits for them, and re-layouts  30.8 us (16%)
  matrix products  14.2 us (8%)
  starting transfers between devices  9.41 us (5%)
  other arithmetic  6.56 us (3%)
    ppermute x2, waiting for transfers between devices, from_partner(): return lax.ppermute(value, axis, pairs)  71.4 us
    all_to_all x1, waiting for transfers between devices, body(): lax.all_to_all(coeffs.reshape(box_size, group_size, rank, shots), 'box',...  55.7 us
    unnamed x18, local copies, waits for them, and re-layouts  8.81 us
    select_n x2, other arithmetic, body(): first_child = jnp.where(upper_half, partner_coeffs, coeffs)  6.51 us
    all_to_all x1, starting transfers between devices, body(): lax.all_to_all(coeffs.reshape(box_size, group_size, rank, shots), 'box',...  6.1 us
    gather x3, local copies, waits for them, and re-layouts, body(): couplings[level_row][kind_rows]  5.86 us
    reshape x1, local copies, waits for them, and re-layouts, body(): basis_in.reshape(box_count, points, rank)  4.77 us
    dot_general x2, matrix products, body(): jnp.einsum('kij,kjs->kis', weights, stacked, preferred_element_type=jnp.f...  4.68 us
  transfers between devices with their start and end apart: 3, of which 3 were waited for; matrix products, arithmetic and copies ran while one was open for 9% of the time, Pallas kernels for 0%

commit v1 on v0

v1 whole, which is shorter than its diff:
```python
import functools

import jax
import jax.numpy as jnp
from jax import lax
from jax.experimental import pallas as pl
from jax.experimental.pallas import tpu as pltpu
from jax.sharding import PartitionSpec as P

MESH = pl.DeviceIdType.MESH


def dot(left, right):
    return jnp.dot(left, right, preferred_element_type=jnp.float32).astype(jnp.bfloat16)


def for_nodes(count, step, run):
    step = min(step, count)
    if step == count:
        for node in range(count):
            run(node)
        return

    def several(outer, carry):
        for inner in range(step):
            run(outer * step + inner)
        return carry

    lax.fori_loop(0, count // step, several, 0)


def kernel(
    pair_size, box_size, rank,
    sources, basis_in, kinds, couplings, basis_out, wavefield,
    shots_in, bases_in, bases_out, last, moved, work, field,
    *rest,
):
    pair_levels = pair_size.bit_length() - 1
    box_levels = box_size.bit_length() - 1
    stacks = rest[:pair_levels]
    in_sem, vin_sem, uin_sem, out_sem, pair_send, pair_recv, box_send, box_recv = rest[pair_levels:]
    pair = lax.axis_index("pair")
    box = lax.axis_index("box")
    chunks = shots_in.shape[0]

    def load_shots(j):
        return pltpu.make_async_copy(sources.at[:, j], shots_in.at[j], in_sem.at[j])

    def load_in(j):
        return pltpu.make_async_copy(basis_in.at[:, j], bases_in.at[j], vin_sem.at[j])

    def load_out(j):
        return pltpu.make_async_copy(basis_out.at[:, j], bases_out.at[j], uin_sem.at[j])

    def store(j):
        return pltpu.make_async_copy(field.at[j], wavefield.at[:, j], out_sem.at[j])

    def half(level):
        bit = lax.rem(pair // 2**level, 2)
        return bit, pl.ds(pl.multiple_of(bit * rank, rank), rank)

    def partner(level):
        bit, _ = half(level)
        return pair + 2**level * (1 - 2 * bit)

    def exchange(level, j):
        _, rows = half(level)
        return pltpu.make_async_remote_copy(
            src_ref=stacks[level].at[j, :, rows],
            dst_ref=stacks[level].at[j, :, rows],
            send_sem=pair_send.at[level, j],
            recv_sem=pair_recv.at[level, j],
            device_id=(partner(level), box),
            device_id_type=MESH,
        )

    def peer(step):
        return lax.rem(box + step, box_size)

    def scatter(j, step):
        return pltpu.make_async_remote_copy(
            src_ref=last.at[j, peer(step)],
            dst_ref=moved.at[j, box],
            send_sem=box_send.at[j, step],
            recv_sem=box_recv.at[j, step],
            device_id=(pair, peer(step)),
            device_id_type=MESH,
        )

    def each_peer(run):
        def one(step, carry):
            run(step)
            return carry

        lax.fori_loop(1, box_size, one, 0)

    def first(j):
        load_shots(j).wait()
        load_in(j).wait()
        _, rows = half(0)

        def node(g):
            product = lax.dot_general(
                bases_in[j, g], shots_in[j, g], (((0,), (0,)), ((), ())),
                preferred_element_type=jnp.float32,
            )
            stacks[0][j, g, rows] = product.astype(jnp.bfloat16)

        for_nodes(box_size, 8, node)
        exchange(0, j).start()

    def pair_level(level, j):
        exchange(level, j).wait_recv()
        final = level == pair_levels - 1
        if not final:
            _, rows = half(level + 1)

        def node(g):
            weights = couplings[level, kinds[level, g * chunks + j]]
            value = dot(weights, stacks[level][j, g])
            if final:
                last[j, g] = value
            else:
                stacks[level + 1][j, g, rows] = value

        for_nodes(box_size, 8, node)
        if final:
            each_peer(lambda step: scatter(j, step).start())
            moved[j, box] = last[j, box]
        else:
            exchange(level + 1, j).start()

    def box_stage(j):
        load_out(j).wait()
        each_peer(lambda step: scatter(j, step).wait_recv())
        for depth in range(box_levels):
            stride = 2**depth
            row = pair_levels + depth

            def pair_of(index):
                low = index // stride * (2 * stride) + index % stride
                high = low + stride
                if depth == 0:
                    one, two = moved[j, low], moved[j, high]
                else:
                    one, two = work[depth - 1, low], work[depth - 1, high]
                stack = jnp.concatenate([one, two], axis=0)
                weights = jnp.concatenate(
                    [
                        couplings[row, kinds[row, low * chunks + j]],
                        couplings[row, kinds[row, high * chunks + j]],
                    ],
                    axis=0,
                )
                value = dot(weights, stack)
                work[depth, low] = value[:rank]
                work[depth, high] = value[rank:]

            for_nodes(box_size // 2, 4, pair_of)

        def node(b):
            field[j, b] = dot(bases_out[j, b], work[box_levels - 1, b])

        for_nodes(box_size, 8, node)
        store(j).start()

    def each_chunk(run):
        def one(j, carry):
            run(j)
            return carry

        lax.fori_loop(0, chunks, one, 0)

    def load(j):
        load_shots(j).start()
        load_in(j).start()

    each_chunk(load)
    each_chunk(lambda j: load_out(j).start())

    barrier = pltpu.get_barrier_semaphore()
    for level in range(pair_levels):
        pl.semaphore_signal(barrier, inc=1, device_id=(partner(level), box), device_id_type=MESH)

    def greet(step):
        pl.semaphore_signal(barrier, inc=1, device_id=(pair, peer(step)), device_id_type=MESH)

    each_peer(greet)
    pl.semaphore_wait(barrier, pair_levels + box_size - 1)

    starts = [0, 1]
    for level in range(1, pair_levels):
        starts.append(starts[-1] + 2)
    starts.append(starts[-1] + 2)

    def iteration(i, carry):
        def at(start, run):
            j = i - start

            @pl.when(jnp.logical_and(j >= 0, j < chunks))
            def _():
                run(j)

        at(starts[0], first)
        for level in range(pair_levels):
            at(starts[1 + level], functools.partial(pair_level, level))
        at(starts[-1], box_stage)
        return carry

    lax.fori_loop(0, chunks + starts[-1], iteration, 0)

    def finish(j):
        store(j).wait()
        for level in range(pair_levels):
            exchange(level, j).wait_send()
        each_peer(lambda step: scatter(j, step).wait_send())

    each_chunk(finish)


def body(sources, basis_in, kinds, couplings, basis_out):
    pair_size = lax.axis_size("pair")
    box_size = lax.axis_size("box")
    box_count, points, shots = sources.shape
    rank = couplings.shape[2]
    pair_levels = pair_size.bit_length() - 1
    box_levels = box_size.bit_length() - 1
    chunks = box_count // box_size
    dtype = jnp.bfloat16
    block = (chunks, box_size, rank, shots)
    any_space = pl.BlockSpec(memory_space=pl.ANY)
    wavefield = pl.pallas_call(
        functools.partial(kernel, pair_size, box_size, rank),
        out_shape=jax.ShapeDtypeStruct((box_size, chunks, points, shots), dtype),
        in_specs=[
            any_space,
            any_space,
            pl.BlockSpec(memory_space=pltpu.SMEM),
            pl.BlockSpec(memory_space=pltpu.VMEM),
            any_space,
        ],
        out_specs=any_space,
        scratch_shapes=[
            pltpu.VMEM((chunks, box_size, points, shots), dtype),
            pltpu.VMEM((chunks, box_size, points, rank), dtype),
            pltpu.VMEM((chunks, box_size, points, rank), dtype),
            pltpu.VMEM(block, dtype),
            pltpu.VMEM(block, dtype),
            pltpu.VMEM((box_levels, box_size, rank, shots), dtype),
            pltpu.VMEM((chunks, box_size, points, shots), dtype),
        ]
        + [pltpu.VMEM((chunks, box_size, 2 * rank, shots), dtype)] * pair_levels
        + [pltpu.SemaphoreType.DMA((chunks,))] * 4
        + [pltpu.SemaphoreType.DMA((pair_levels, chunks))] * 2
        + [pltpu.SemaphoreType.DMA((chunks, box_size))] * 2,
        compiler_params=pltpu.CompilerParams(
            collective_id=0, has_side_effects=True, vmem_limit_bytes=56 * 2**20
        ),
    )(
        sources.reshape(box_size, chunks, points, shots),
        basis_in.reshape(box_size, chunks, points, rank),
        kinds,
        couplings,
        basis_out.reshape(box_size, chunks, points, rank),
    )
    return wavefield.reshape(box_count, points, shots)


def solution(mesh):
    in_specs = (
        P(("pair", "box"), None, None),
        P(("pair", "box"), None),
        P(None, ("pair", "box")),
        P(),
        P(("pair", "box"), None),
    )
    out_specs = P(("pair", "box"), None, None)
    return jax.shard_map(body, mesh=mesh, in_specs=in_specs, out_specs=out_specs, check_vma=False)
```

time: 189 us -> 99.6 us (0.53)
  waiting for transfers between devices: 127 us -> 0 us
  Pallas kernels: 0 us -> 88.6 us
  local copies, waits for them, and re-layouts: 30.8 us -> 10.8 us
  matrix products: 14.2 us -> 0 us
  starting transfers between devices: 9.41 us -> 0 us
  other arithmetic: 6.56 us -> 0 us
    pallas_call x0 -> x1, Pallas kernels: none -> 88.6 us  [body(): pl.pallas_call(functools.partial(kernel, pair_size, box_size, rank), out_...]
    ppermute x2 -> x0, waiting for transfers between devices: 71.4 us -> none  [from_partner(): return lax.ppermute(value, axis, pairs)]
    all_to_all x1 -> x0, waiting for transfers between devices: 55.7 us -> none  [body(): lax.all_to_all(coeffs.reshape(box_size, group_size, rank, shots), 'box',...]
    dot_general x7 -> x0, matrix products: 14.2 us -> none  [the longest x2 4.68 us: body(): jnp.einsum('kij,kjs->kis', weights, stacked, preferred_element_type=jnp.f...]
    gather x5 -> x0, local copies, waits for them, and re-layouts: 7.55 us -> none  [the longest x3 5.86 us: body(): couplings[level_row][kind_rows]]
    select_n x6 -> x0, other arithmetic: 6.53 us -> none  [the longest x2 6.51 us: body(): first_child = jnp.where(upper_half, partner_coeffs, coeffs)]
    all_to_all x1 -> x0, starting transfers between devices: 6.1 us -> none  [body(): lax.all_to_all(coeffs.reshape(box_size, group_size, rank, shots), 'box',...]
    unnamed x18 -> x1, local copies, waits for them, and re-layouts: 8.81 us -> 3.97 us
  transfers between devices with their start and end apart: 3 -> 0, of which waited for: 3 -> 0; matrix products, arithmetic and copies ran while one was open for 9% -> 0% of each run, Pallas kernels for 0% -> 0%
where the time goes in v1:
time: 99.6 us; the launch traced here: 99.4 us
  Pallas kernels  88.6 us (89%)
  local copies, waits for them, and re-layouts  10.8 us (11%)
    pallas_call x1, Pallas kernels, body(): pl.pallas_call(functools.partial(kernel, pair_size, box_size, rank), out_...  88.6 us
    unnamed x1, local copies, waits for them, and re-layouts  3.97 us
    reshape x1, local copies, waits for them, and re-layouts, body(): basis_in.reshape(box_size, chunks, points, rank)  3.41 us
    reshape x1, local copies, waits for them, and re-layouts, body(): basis_out.reshape(box_size, chunks, points, rank)  3.41 us

profile of v1, /device:TPU:0, one launch (start us, length us, event | category | flops | bytes accessed | tf_op | source)
XLA Modules:
  0.0 99.4 jit_solution(9385258173833247187)
XLA Ops:
  0.0 3.4 %reshape.13.basis_in = bf16[8,12,64,64]{3,2,1,0:T(8,128)(2,1)} reshape(bf16[96,4096]{1,0:T(8,128)(2,1)} %param.6) | data formatting | bytes 1572864 | tf_op jit(solution)/shard_map/reshape | solution.py:261
  3.4 3.4 %reshape.14.basis_out = bf16[8,12,64,64]{3,2,1,0:T(8,128)(2,1)} reshape(bf16[96,4096]{1,0:T(8,128)(2,1)} %param.9) | data formatting | bytes 1572864 | tf_op jit(solution)/shard_map/reshape | solution.py:264
  6.8 88.6 %shard_map.55 = bf16[8,12,64,256]{3,2,1,0:T(8,128)(2,1)} custom-call(bf16[8,12,64,256]{3,2,1,0:T(8,128)(2,1)} %bitcast.3, bf16[8,12,64,64]{3,2,1,0:T(8,128)(2,1)} %reshape.13.basis_in, s32[5,96]{1,0:T(8,128)} %kinds.1, bf16[5,8,64,128]{3,2,1,0:T(8,128)(2,1)} %couplings.1, bf16[8,12,64,64]{3,2,1,0:T(8,128)(2,1)} %reshape.14.basis_out), custom_call_target="tpu_custom_call" | custom-call | tf_op jit(solution)/shard_map/pallas_call | solution.py:232
  95.4 4.0 %copy.7 = bf16[96,64,256]{2,1,0:T(8,128)(2,1)} copy(bf16[96,64,256]{2,1,0:T(8,128)(2,1)} %bitcast.2) | data formatting | bytes 6291456
